TPU v7x, 512 devices: a whole 4x8x8 slice. The times are simulated.
512 devices in a mesh: chain: 64 (over y, x, core), cols: 8 (over z).
Axes of the slice: x: 4, y: 8, z: 8, core: 2. Of those that a mesh axis runs over, the one named last changes fastest.
Arguments:
- start_vectors: float32 [1024, 256, 256], P('chain', 'cols'), may hold values from -6 to 6
- factors: float32 [1024, 256, 256], P('chain', 'cols'), may hold values from -1.2 to 1.2, as said below
Outputs:
- vectors: float32 [1024, 256, 256], P('chain', 'cols')
- log_growth: float32 [256], P('cols')
Inputs may be any that keep to these rules, and one draw needn't show every extreme that they name: `factors`: the factor blocks of the shifted operator; every product of consecutive factor blocks is bounded.
All inputs are finite; a program needn't handle non-finite values.
Results may differ from a plain program's by a relative error of at most 0.0003.
Values sent between devices are 32-bit elements; how exact they have to be, the bound alone decides.
No kernel may reach another device: no remote copies, remote signals or barrier semaphores. Data moves between devices by JAX's collectives and lax.ppermute only.
A program may use at most 128 MiB of HBM per device.

v0:
```python
import jax
import jax.numpy as jnp
from jax import lax
from jax.sharding import PartitionSpec as P

eps_value = 1e-06


def from_behind(block, axis, distance):
    devices = range(lax.axis_size(axis))
    route = [(i - distance, i) for i in devices if i - distance in devices]
    return lax.ppermute(block, axis, route)


def transform(matrix, vectors_in):
    return lax.dot_general(
        vectors_in,
        matrix,
        (((1,), (1,)), ((), ())),
        precision=lax.Precision.HIGHEST,
        preferred_element_type=jnp.float32,
    )


def compose(later, earlier):
    return jnp.dot(
        later, earlier, precision=lax.Precision.HIGHEST, preferred_element_type=jnp.float32
    )


def forward_rows(factors, right_side, incoming):

    def forward_advance(carried, element):
        matrix, source = element
        carried = transform(matrix, carried) + source
        return (carried, carried)

    return lax.scan(forward_advance, incoming, (factors, right_side))


def backward_rows(factors, forward, incoming):

    def backward_advance(carried, element):
        matrix, source = element
        carried = transform(matrix, source + carried)
        return (carried, carried)

    return lax.scan(backward_advance, incoming, (factors, forward), reverse=True)


def chain_operator(factors, reverse):
    identity_block = jnp.eye(factors.shape[1], dtype=jnp.float32)

    def chain_advance(running, matrix):
        return (compose(matrix, running), None)

    running, _ = lax.scan(chain_advance, identity_block, factors, reverse=reverse)
    return running


def section_count():
    return (lax.axis_size("chain") - 1).bit_length()


def enter_state(summary, direction):
    return from_behind(summary, "chain", direction)


def solve_system(factors, right_side, prefix_forward, prefix_backward):
    zero_state = jnp.zeros(right_side.shape[1:], jnp.float32)
    local_last, _ = forward_rows(factors, right_side, zero_state)
    incoming = enter_state(prefix_forward(local_last), 1)
    _, forward = forward_rows(factors, right_side, incoming)
    local_first, _ = backward_rows(factors, forward, zero_state)
    incoming_back = enter_state(prefix_backward(local_first), -1)
    _, solved = backward_rows(factors, forward, incoming_back)
    return solved


def shards(start_vectors, factors):
    full_factors = lax.all_gather(factors, "cols", axis=1, tiled=True)

    def pair_prefix(operator, summary, direction):
        sections = section_count()
        for section_index in range(sections):
            distance = direction * (1 << section_index)
            if section_index + 1 < sections:
                received_op, received_sum = from_behind((operator, summary), "chain", distance)
                summary = transform(operator, received_sum) + summary
                operator = compose(operator, received_op)
            else:
                received_sum = from_behind(summary, "chain", distance)
                summary = transform(operator, received_sum) + summary
        return summary

    def prefix_forward(summary):
        return pair_prefix(chain_operator(full_factors, False), summary, 1)

    def prefix_backward(summary):
        return pair_prefix(chain_operator(full_factors, True), summary, -1)

    cell_count = start_vectors.shape[0] * lax.axis_size("chain") * start_vectors.shape[2]
    first_solve = solve_system(full_factors, start_vectors, prefix_forward, prefix_backward)
    first_squares = lax.psum(jnp.sum(first_solve * first_solve, axis=(0, 2)), "chain")
    scale_one = jnp.sqrt(first_squares / cell_count + eps_value)
    second_solve = solve_system(
        full_factors, first_solve / scale_one[None, :, None], prefix_forward, prefix_backward
    )
    second_squares = lax.psum(jnp.sum(second_solve * second_solve, axis=(0, 2)), "chain")
    scale_two = jnp.sqrt(second_squares / cell_count + eps_value)
    result_vectors = second_solve / scale_two[None, :, None]
    return (result_vectors, jnp.log(scale_two))


def solution(mesh):
    return jax.shard_map(
        shards,
        mesh=mesh,
        in_specs=(P("chain", "cols", None), P("chain", "cols", None)),
        out_specs=(P("chain", "cols", None), P("cols")),
        check_vma=False,
    )
```

profile of v0, /device:TPU:32, one launch (start us, length us, event | category | flops | bytes accessed | tf_op | source)
XLA Modules:
  0.0 812.4 jit_solution(6026892274242298097)
XLA Ops:
  8.0 64.7 %all-gather.2.cloned.1.call-done = f32[16,256,256]{2,1,0:T(8,128)} async-done(((f32[16,32,256]{2,1,0:T(8,128)}), f32[16,256,256]{2,1,0:T(8,128)}) %all-gather.2.cloned.1.call-update) | async-done | bytes 4194320 | tf_op jit(solution)/shard_map/all_gather | solution.py:81
  72.7 21.4 %while.146 = (s32[]{:T(128)}, f32[32,256]{1,0:T(8,128)S(1)}, f32[16,256,256]{2,1,0:T(8,128)}, f32[16,32,256]{2,1,0:T(8,128)}, s32[]{:T(128)}, /*index=5*/s32[]{:T(128)}) while((s32[]{:T(128)}, f32[32,256]{1,0:T(8,128)S(1)}, f32[16,256,256]{2,1,0:T(8,128)}, f32[16,32,256]{2,1,0:T(8,128)}, s32[]{:T(128)}, /*index=5*/s32[]{:T(128)}) %tuple.241), condition=%wide.region_1.2_spmd.clone, body=%wide.region_0.1_spmd.clone.sunk | while | flops 25182212 | bytes 427087 | solution.py:38
  96.0 22.1 %while.138 = (s32[]{:T(128)}, f32[256,256]{1,0:T(8,128)S(1)}, f32[16,256,256]{2,1,0:T(8,128)}, s32[]{:T(128)}) while((s32[]{:T(128)}, f32[256,256]{1,0:T(8,128)S(1)}, f32[16,256,256]{2,1,0:T(8,128)}, s32[]{:T(128)}) %tuple.273), condition=%wide.region_3.4_spmd, body=%wide.region_2.3_spmd.sunk | while | flops 201326592 | bytes 1311285 | solution.py:57
  134.6 7.3 collective-permute-done.4
  146.4 10.8 %collective-permute-done.6 = f32[256,256]{1,0:T(8,128)S(1)} collective-permute-done((f32[256,256]{1,0:T(8,128)S(1)}, f32[256,256]{1,0:T(8,128)S(1)}, u32[]{:S(2)}, u32[]{:S(2)}) %collective-permute-start.6) | collective-permute-done | bytes 262176 | tf_op jit(solution)/shard_map/ppermute | solution.py:12
  161.9 7.5 collective-permute-done.8
  173.3 7.5 collective-permute-done.10
  190.7 21.4 %while.139 = (s32[]{:T(128)}, f32[32,256]{1,0:T(8,128)S(1)}, f32[16,32,256]{2,1,0:T(8,128)S(1)}, f32[16,256,256]{2,1,0:T(8,128)}, f32[16,32,256]{2,1,0:T(8,128)}, /*index=5*/s32[]{:T(128)}) while((s32[]{:T(128)}, f32[32,256]{1,0:T(8,128)S(1)}, f32[16,32,256]{2,1,0:T(8,128)S(1)}, f32[16,256,256]{2,1,0:T(8,128)}, f32[16,32,256]{2,1,0:T(8,128)}, ...), condition=%wide.region_5.6_spmd, body=%wide.region_4.5_spmd.sunk | while | flops 25174016 | bytes 459845 | solution.py:38
  212.1 21.3 %while.140 = (s32[]{:T(128)}, f32[32,256]{1,0:T(8,128)S(1)}, f32[16,32,256]{2,1,0:T(8,128)S(1)}, f32[16,256,256]{2,1,0:T(8,128)}, s32[]{:T(128)}, /*index=5*/s32[]{:T(128)}) while((s32[]{:T(128)}, f32[32,256]{1,0:T(8,128)S(1)}, f32[16,32,256]{2,1,0:T(8,128)S(1)}, f32[16,256,256]{2,1,0:T(8,128)}, s32[]{:T(128)}, /*index=5*/s32[]{:T(128)}) %tuple.275), condition=%wide.region_7.8_spmd, body=%wide.region_6.7_spmd.sunk | while | flops 25174020 | bytes 427089 | solution.py:48
  235.4 22.1 %while.141 = (s32[]{:T(128)}, f32[256,256]{1,0:T(8,128)S(1)}, f32[16,256,256]{2,1,0:T(8,128)}, s32[]{:T(128)}, s32[]{:T(128)}) while((s32[]{:T(128)}, f32[256,256]{1,0:T(8,128)S(1)}, f32[16,256,256]{2,1,0:T(8,128)}, s32[]{:T(128)}, s32[]{:T(128)}) %tuple.276), condition=%wide.region_9.10_spmd, body=%wide.region_8.9_spmd.sunk | while | flops 201326592 | bytes 1310797 | solution.py:57
  278.5 7.5 collective-permute-done.18
  290.7 6.7 collective-permute-done.20
  301.4 13.4 %collective-permute-done.22 = f32[256,256]{1,0:T(8,128)S(1)} collective-permute-done((f32[256,256]{1,0:T(8,128)S(1)}, f32[256,256]{1,0:T(8,128)S(1)}, u32[]{:S(2)}, u32[]{:S(2)}) %collective-permute-start.22) | collective-permute-done | bytes 262176 | tf_op jit(solution)/shard_map/ppermute | solution.py:12
  322.7 21.6 %while.142 = (s32[]{:T(128)}, f32[32,256]{1,0:T(8,128)S(1)}, f32[16,32,256]{2,1,0:T(8,128)S(1)}, f32[16,32,256]{2,1,0:T(8,128)}, f32[16,256,256]{2,1,0:T(8,128)}, /*index=5*/s32[]{:T(128)}, s32[]{:T(128)}) while((s32[]{:T(128)}, f32[32,256]{1,0:T(8,128)S(1)}, f32[16,32,256]{2,1,0:T(8,128)S(1)}, f32[16,32,256]{2,1,0:T(8,128)}, ...), condition=%wide.region_11.12_spmd, body=%wide.region_10.11_spmd.sunk | while | flops 25174020 | bytes 460377 | solution.py:48
  344.5 129.1 %psum.14 = f32[32]{0:T(128)S(1)} all-reduce(f32[32]{0:T(128)S(1)} %multiply_reduce_fusion.1), channel_id=1, replica_groups=mesh['chain'=64,'cols'=8] {'chain'}, use_global_device_ids=true, to_apply=%region_13.14 | all-reduce | flops 32 | bytes 256 | tf_op jit(solution)/shard_map/psum | solution.py:104
  474.5 21.5 %while.147 = (s32[]{:T(128)}, f32[32,256]{1,0:T(8,128)S(1)}, f32[16,256,256]{2,1,0:T(8,128)}, f32[16,32,256]{2,1,0:T(8,128)}, s32[]{:T(128)}, /*index=5*/s32[]{:T(128)}) while((s32[]{:T(128)}, f32[32,256]{1,0:T(8,128)S(1)}, f32[16,256,256]{2,1,0:T(8,128)}, f32[16,32,256]{2,1,0:T(8,128)}, s32[]{:T(128)}, ...), condition=%wide.region_15.16_spmd.clone, body=%wide.region_14.15_spmd.clone.sunk | while | flops 25182212 | bytes 427087 | solution.py:38
  506.8 7.2 collective-permute-done.25
  516.4 7.5 collective-permute-done.26
  541.4 8.2 %collective-permute-done.29 = f32[32,256]{1,0:T(8,128)S(1)} collective-permute-done((f32[32,256]{1,0:T(8,128)S(1)}, f32[32,256]{1,0:T(8,128)S(1)}, u32[]{:S(2)}, u32[]{:S(2)}) %collective-permute-start.29) | collective-permute-done | bytes 32800 | tf_op jit(solution)/shard_map/ppermute | solution.py:12
  558.6 21.4 %while.143 = (s32[]{:T(128)}, f32[32,256]{1,0:T(8,128)S(1)}, f32[16,32,256]{2,1,0:T(8,128)S(1)}, f32[16,256,256]{2,1,0:T(8,128)}, f32[16,32,256]{2,1,0:T(8,128)}, /*index=5*/s32[]{:T(128)}) while((s32[]{:T(128)}, f32[32,256]{1,0:T(8,128)S(1)}, f32[16,32,256]{2,1,0:T(8,128)S(1)}, f32[16,256,256]{2,1,0:T(8,128)}, f32[16,32,256]{2,1,0:T(8,128)}, ...), condition=%wide.region_17.18_spmd, body=%wide.region_16.17_spmd.sunk | while | flops 25174016 | bytes 459845 | solution.py:38
  580.0 21.3 %while.144 = (s32[]{:T(128)}, f32[32,256]{1,0:T(8,128)S(1)}, f32[16,32,256]{2,1,0:T(8,128)S(1)}, f32[16,256,256]{2,1,0:T(8,128)}, s32[]{:T(128)}, /*index=5*/s32[]{:T(128)}) while((s32[]{:T(128)}, f32[32,256]{1,0:T(8,128)S(1)}, f32[16,32,256]{2,1,0:T(8,128)S(1)}, f32[16,256,256]{2,1,0:T(8,128)}, s32[]{:T(128)}, /*index=5*/s32[]{:T(128)}) %tuple.280), condition=%wide.region_19.20_spmd, body=%wide.region_18.19_spmd.sunk | while | flops 25174020 | bytes 427089 | solution.py:48
  635.6 16.2 %collective-permute-start.37 = (f32[32,256]{1,0:T(8,128)S(1)}, f32[32,256]{1,0:T(8,128)S(1)}, u32[]{:S(2)}, u32[]{:S(2)}) collective-permute-start(f32[32,256]{1,0:T(8,128)S(1)} %convolution_add_fusion), channel_id=1, source_target_pairs={{8,0},{16,8},{24,16},{32,24},{40,32},{48,40},{56,48},{64,56},{72,6... | collective-permute-start | bytes 98312 | tf_op jit(solution)/shard_map/ppermute | solution.py:12
  653.5 21.3 %while.145 = (s32[]{:T(128)}, f32[32,256]{1,0:T(8,128)S(1)}, f32[16,32,256]{2,1,0:T(8,128)S(1)}, f32[16,32,256]{2,1,0:T(8,128)S(1)}, f32[16,256,256]{2,1,0:T(8,128)}, /*index=5*/s32[]{:T(128)}, s32[]{:T(128)}) while((s32[]{:T(128)}, f32[32,256]{1,0:T(8,128)S(1)}, f32[16,32,256]{2,1,0:T(8,128)S(1)}, f32[16,32,256]{2,1,0:T(8,128)S(1)}, ...), condition=%wide.region_21.22_spmd, body=%wide.region_20.21_spmd.sunk | while | flops 25174020 | bytes 460377 | solution.py:48
  675.0 129.1 %psum.15 = f32[32]{0:T(128)S(1)} all-reduce(f32[32]{0:T(128)S(1)} %multiply_reduce_fusion), channel_id=1, replica_groups=mesh['chain'=64,'cols'=8] {'chain'}, use_global_device_ids=true, to_apply=%region_23.24 | all-reduce | flops 32 | bytes 256 | tf_op jit(solution)/shard_map/psum | solution.py:109
  (443 shorter events, 369.9 us)
Async XLA Ops:
  7.2 65.5 %all-gather.2.cloned.1.call-start = ((), (), s32[]{:S(2)}) async-start(), calls=%async_computation | async-start | bytes 4718592 | tf_op jit(solution)/shard_map/all_gather | solution.py:81
  94.1 27.5 %collective-permute-start = (f32[32,256]{1,0:T(8,128)S(1)}, f32[32,256]{1,0:T(8,128)S(1)}, u32[]{:S(2)}, u32[]{:S(2)}) collective-permute-start(f32[32,256]{1,0:T(8,128)S(1)} %get-tuple-element.568), channel_id=1, source_target_pairs={{0,8},{8,16},{16,24},{24,32},{32,40},{40,48},{48,56},{56,64},{64,7... | collective-permute-start | bytes 98312 | tf_op jit(solution)/shard_map/ppermute | solution.py:12
  118.1 11.0 %collective-permute-start.2 = (f32[256,256]{1,0:T(8,128)S(1)}, f32[256,256]{1,0:T(8,128)S(1)}, u32[]{:S(2)}, u32[]{:S(2)}) collective-permute-start(f32[256,256]{1,0:T(8,128)S(1)} %get-tuple-element.569), channel_id=1, source_target_pairs={{0,8},{8,16},{16,24},{24,32},{32,40},{40,48},{48,56},{56,64},{64,7... | collective-permute-start | bytes 786440 | tf_op jit(solution)/shard_map/ppermute | solution.py:12
  122.0 9.5 %collective-permute-start.1 = (f32[32,256]{1,0:T(8,128)S(1)}, f32[32,256]{1,0:T(8,128)S(1)}, u32[]{:S(2)}, u32[]{:S(2)}) collective-permute-start(f32[32,256]{1,0:T(8,128)S(1)} %convolution_add_fusion.23), channel_id=1, source_target_pairs={{0,16},{8,24},{16,32},{24,40},{32,48},{40,56},{48,64},{56,72},{64,... | collective-permute-start | bytes 98312 | tf_op jit(solution)/shard_map/ppermute | solution.py:12
  129.5 12.3 %collective-permute-start.4 = (f32[256,256]{1,0:T(8,128)S(1)}, f32[256,256]{1,0:T(8,128)S(1)}, u32[]{:S(2)}, u32[]{:S(2)}) collective-permute-start(f32[256,256]{1,0:T(8,128)S(1)} %fusion.54), channel_id=1, source_target_pairs={{0,16},{8,24},{16,32},{24,40},{32,48},{40,56},{48,64},{56,72},{64,... | collective-permute-start | bytes 786440 | tf_op jit(solution)/shard_map/ppermute | solution.py:12
  131.8 12.3 %collective-permute-start.3 = (f32[32,256]{1,0:T(8,128)S(1)}, f32[32,256]{1,0:T(8,128)S(1)}, u32[]{:S(2)}, u32[]{:S(2)}) collective-permute-start(f32[32,256]{1,0:T(8,128)S(1)} %convolution_add_fusion.22), channel_id=1, source_target_pairs={{0,32},{8,40},{16,48},{24,56},{32,64},{40,72},{48,80},{56,88},{64,... | collective-permute-start | bytes 98312 | tf_op jit(solution)/shard_map/ppermute | solution.py:12
  142.2 15.0 %collective-permute-start.6 = (f32[256,256]{1,0:T(8,128)S(1)}, f32[256,256]{1,0:T(8,128)S(1)}, u32[]{:S(2)}, u32[]{:S(2)}) collective-permute-start(f32[256,256]{1,0:T(8,128)S(1)} %fusion.55), channel_id=1, source_target_pairs={{0,32},{8,40},{16,48},{24,56},{32,64},{40,72},{48,80},{56,88},{64,... | collective-permute-start | bytes 786440 | tf_op jit(solution)/shard_map/ppermute | solution.py:12
  144.5 15.1 %collective-permute-start.5 = (f32[32,256]{1,0:T(8,128)S(1)}, f32[32,256]{1,0:T(8,128)S(1)}, u32[]{:S(2)}, u32[]{:S(2)}) collective-permute-start(f32[32,256]{1,0:T(8,128)S(1)} %convolution_add_fusion.21), channel_id=1, source_target_pairs={{0,64},{8,72},{16,80},{24,88},{32,96},{40,104},{48,112},{56,120},{... | collective-permute-start | bytes 98312 | tf_op jit(solution)/shard_map/ppermute | solution.py:12
  157.6 11.7 %collective-permute-start.8 = (f32[256,256]{1,0:T(8,128)S(1)}, f32[256,256]{1,0:T(8,128)S(1)}, u32[]{:S(2)}, u32[]{:S(2)}) collective-permute-start(f32[256,256]{1,0:T(8,128)S(1)} %fusion.56), channel_id=1, source_target_pairs={{0,64},{8,72},{16,80},{24,88},{32,96},{40,104},{48,112},{56,120},{... | collective-permute-start | bytes 786440 | tf_op jit(solution)/shard_map/ppermute | solution.py:12
  159.9 11.7 %collective-permute-start.7 = (f32[32,256]{1,0:T(8,128)S(1)}, f32[32,256]{1,0:T(8,128)S(1)}, u32[]{:S(2)}, u32[]{:S(2)}) collective-permute-start(f32[32,256]{1,0:T(8,128)S(1)} %convolution_add_fusion.20), channel_id=1, source_target_pairs={{0,128},{8,136},{16,144},{24,152},{32,160},{40,168},{48,176},{56,1... | collective-permute-start | bytes 98312 | tf_op jit(solution)/shard_map/ppermute | solution.py:12
  169.7 11.1 %collective-permute-start.10 = (f32[256,256]{1,0:T(8,128)S(1)}, f32[256,256]{1,0:T(8,128)S(1)}, u32[]{:S(2)}, u32[]{:S(2)}) collective-permute-start(f32[256,256]{1,0:T(8,128)S(1)} %fusion.57), channel_id=1, source_target_pairs={{0,128},{8,136},{16,144},{24,152},{32,160},{40,168},{48,176},{56,1... | collective-permute-start | bytes 786440 | tf_op jit(solution)/shard_map/ppermute | solution.py:12
  172.0 9.7 %collective-permute-start.9 = (f32[32,256]{1,0:T(8,128)S(1)}, f32[32,256]{1,0:T(8,128)S(1)}, u32[]{:S(2)}, u32[]{:S(2)}) collective-permute-start(f32[32,256]{1,0:T(8,128)S(1)} %convolution_add_fusion.19), channel_id=1, source_target_pairs={{0,256},{8,264},{16,272},{24,280},{32,288},{40,296},{48,304},{56,3... | collective-permute-start | bytes 98312 | tf_op jit(solution)/shard_map/ppermute | solution.py:12
  233.5 26.0 %collective-permute-start.12 = (f32[32,256]{1,0:T(8,128)S(1)}, f32[32,256]{1,0:T(8,128)S(1)}, u32[]{:S(2)}, u32[]{:S(2)}) collective-permute-start(f32[32,256]{1,0:T(8,128)S(1)} %get-tuple-element.571), channel_id=1, source_target_pairs={{8,0},{16,8},{24,16},{32,24},{40,32},{48,40},{56,48},{64,56},{72,6... | collective-permute-start | bytes 98312 | tf_op jit(solution)/shard_map/ppermute | solution.py:12
  264.1 9.8 %collective-permute-start.16 = (f32[256,256]{1,0:T(8,128)S(1)}, f32[256,256]{1,0:T(8,128)S(1)}, u32[]{:S(2)}, u32[]{:S(2)}) collective-permute-start(f32[256,256]{1,0:T(8,128)S(1)} %fusion.59), channel_id=1, source_target_pairs={{16,0},{24,8},{32,16},{40,24},{48,32},{56,40},{64,48},{72,56},{80,... | collective-permute-start | bytes 786440 | tf_op jit(solution)/shard_map/ppermute | solution.py:12
  266.9 9.2 %collective-permute-start.15 = (f32[32,256]{1,0:T(8,128)S(1)}, f32[32,256]{1,0:T(8,128)S(1)}, u32[]{:S(2)}, u32[]{:S(2)}) collective-permute-start(f32[32,256]{1,0:T(8,128)S(1)} %convolution_add_fusion.16), channel_id=1, source_target_pairs={{32,0},{40,8},{48,16},{56,24},{64,32},{72,40},{80,48},{88,56},{96,... | collective-permute-start | bytes 98312 | tf_op jit(solution)/shard_map/ppermute | solution.py:12
  274.3 11.7 %collective-permute-start.18 = (f32[256,256]{1,0:T(8,128)S(1)}, f32[256,256]{1,0:T(8,128)S(1)}, u32[]{:S(2)}, u32[]{:S(2)}) collective-permute-start(f32[256,256]{1,0:T(8,128)S(1)} %fusion.60), channel_id=1, source_target_pairs={{32,0},{40,8},{48,16},{56,24},{64,32},{72,40},{80,48},{88,56},{96,... | collective-permute-start | bytes 786440 | tf_op jit(solution)/shard_map/ppermute | solution.py:12
  276.5 11.9 %collective-permute-start.17 = (f32[32,256]{1,0:T(8,128)S(1)}, f32[32,256]{1,0:T(8,128)S(1)}, u32[]{:S(2)}, u32[]{:S(2)}) collective-permute-start(f32[32,256]{1,0:T(8,128)S(1)} %convolution_add_fusion.15), channel_id=1, source_target_pairs={{64,0},{72,8},{80,16},{88,24},{96,32},{104,40},{112,48},{120,56},{... | collective-permute-start | bytes 98312 | tf_op jit(solution)/shard_map/ppermute | solution.py:12
  286.3 11.1 %collective-permute-start.20 = (f32[256,256]{1,0:T(8,128)S(1)}, f32[256,256]{1,0:T(8,128)S(1)}, u32[]{:S(2)}, u32[]{:S(2)}) collective-permute-start(f32[256,256]{1,0:T(8,128)S(1)} %fusion.61), channel_id=1, source_target_pairs={{64,0},{72,8},{80,16},{88,24},{96,32},{104,40},{112,48},{120,56},{... | collective-permute-start | bytes 786440 | tf_op jit(solution)/shard_map/ppermute | solution.py:12
  288.8 11.0 %collective-permute-start.19 = (f32[32,256]{1,0:T(8,128)S(1)}, f32[32,256]{1,0:T(8,128)S(1)}, u32[]{:S(2)}, u32[]{:S(2)}) collective-permute-start(f32[32,256]{1,0:T(8,128)S(1)} %convolution_add_fusion.14), channel_id=1, source_target_pairs={{128,0},{136,8},{144,16},{152,24},{160,32},{168,40},{176,48},{184,... | collective-permute-start | bytes 98312 | tf_op jit(solution)/shard_map/ppermute | solution.py:12
  297.8 17.0 %collective-permute-start.22 = (f32[256,256]{1,0:T(8,128)S(1)}, f32[256,256]{1,0:T(8,128)S(1)}, u32[]{:S(2)}, u32[]{:S(2)}) collective-permute-start(f32[256,256]{1,0:T(8,128)S(1)} %fusion.62), channel_id=1, source_target_pairs={{128,0},{136,8},{144,16},{152,24},{160,32},{168,40},{176,48},{184,... | collective-permute-start | bytes 786440 | tf_op jit(solution)/shard_map/ppermute | solution.py:12
  300.1 15.1 %collective-permute-start.21 = (f32[32,256]{1,0:T(8,128)S(1)}, f32[32,256]{1,0:T(8,128)S(1)}, u32[]{:S(2)}, u32[]{:S(2)}) collective-permute-start(f32[32,256]{1,0:T(8,128)S(1)} %convolution_add_fusion.13), channel_id=1, source_target_pairs={{256,0},{264,8},{272,16},{280,24},{288,32},{296,40},{304,48},{312,... | collective-permute-start | bytes 98312 | tf_op jit(solution)/shard_map/ppermute | solution.py:12
  514.4 9.6 %collective-permute-start.26 = (f32[32,256]{1,0:T(8,128)S(1)}, f32[32,256]{1,0:T(8,128)S(1)}, u32[]{:S(2)}, u32[]{:S(2)}) collective-permute-start(f32[32,256]{1,0:T(8,128)S(1)} %convolution_add_fusion.10), channel_id=1, source_target_pairs={{0,32},{8,40},{16,48},{24,56},{32,64},{40,72},{48,80},{56,88},{64,... | collective-permute-start | bytes 98312 | tf_op jit(solution)/shard_map/ppermute | solution.py:12
  539.9 9.7 %collective-permute-start.29 = (f32[32,256]{1,0:T(8,128)S(1)}, f32[32,256]{1,0:T(8,128)S(1)}, u32[]{:S(2)}, u32[]{:S(2)}) collective-permute-start(f32[32,256]{1,0:T(8,128)S(1)} %convolution_add_fusion.7), channel_id=1, source_target_pairs={{0,256},{8,264},{16,272},{24,280},{32,288},{40,296},{48,304},{56,3... | collective-permute-start | bytes 98312 | tf_op jit(solution)/shard_map/ppermute | solution.py:12
  635.6 17.8 %collective-permute-start.37 = (f32[32,256]{1,0:T(8,128)S(1)}, f32[32,256]{1,0:T(8,128)S(1)}, u32[]{:S(2)}, u32[]{:S(2)}) collective-permute-start(f32[32,256]{1,0:T(8,128)S(1)} %convolution_add_fusion), channel_id=1, source_target_pairs={{8,0},{16,8},{24,16},{32,24},{40,32},{48,40},{56,48},{64,56},{72,6... | collective-permute-start | bytes 98312 | tf_op jit(solution)/shard_map/ppermute | solution.py:12
  (18 other events, 257.0 us)
Sparse Core Ops, SparseCore 0:
  10.1 62.5 all-gather.1
where the time goes:
time: 818 us; the launch traced here: 812 us
  blocking collectives  258 us (32%)
  matrix products  221 us (27%)
  waiting for transfers between devices  214 us (26%)
  starting transfers between devices  95.2 us (12%)
  between operations  14.9 us (2%)
    dot_general x152, matrix products, transform(): lax.dot_general(vectors_in, matrix, (((1,), (1,)), ((), ())), precision=l...  175 us
    ppermute x38, waiting for transfers between devices, from_behind(): return lax.ppermute(block, axis, route)  148 us
    psum x1, blocking collectives, shards(): lax.psum(jnp.sum(second_solve * second_solve, axis=(0, 2)), 'chain')  129 us
    psum x1, blocking collectives, shards(): lax.psum(jnp.sum(first_solve * first_solve, axis=(0, 2)), 'chain')  129 us
    ppermute x38, starting transfers between devices, from_behind(): return lax.ppermute(block, axis, route)  95.2 us
    all_gather x1, waiting for transfers between devices, shards(): full_factors = lax.all_gather(factors, 'cols', axis=1, tiled=True)  64.7 us
    dot_general x42, matrix products, compose(): jnp.dot(later, earlier, precision=lax.Precision.HIGHEST, preferred_elemen...  46.4 us
  transfers between devices with their start and end apart: 39, of which 29 were waited for; matrix products, arithmetic and copies ran while one was open for 6% of the time, Pallas kernels for 0%

commit v1 on v0

--- a/solution.py
+++ b/solution.py
@@ -78,7 +78,9 @@
 
 
 def shards(start_vectors, factors):
-    full_factors = lax.all_gather(factors, "cols", axis=1, tiled=True)
+    full_factors = jnp.concatenate(
+        lax.all_to_all(jnp.stack([factors] * lax.axis_size("cols")), "cols", 0, 0), axis=1
+    )
 
     def pair_prefix(operator, summary, direction):
         sections = section_count()

time: 818 us -> 851 us (1.040)
  waiting for transfers between devices: 214 us -> 244 us
  between operations: 14.9 us -> 1.48 us
  local copies, waits for them, and re-layouts: 1.35 us -> 10.3 us
    all_to_all x0 -> x1, waiting for transfers between devices: none -> 96.2 us  [shards(): lax.all_to_all(jnp.stack([factors] * lax.axis_size('cols')), 'cols', 0, 0)]
    all_gather x1 -> x0, waiting for transfers between devices: 64.7 us -> none  [shards(): full_factors = lax.all_gather(factors, 'cols', axis=1, tiled=True)]
    all_to_all x0 -> x1, starting transfers between devices: none -> 10.3 us  [shards(): lax.all_to_all(jnp.stack([factors] * lax.axis_size('cols')), 'cols', 0, 0)]
where the time goes in v1:
time: 851 us; the launch traced here: 846 us
  blocking collectives  258 us (30%)
  waiting for transfers between devices  244 us (29%)
  matrix products  221 us (26%)
  starting transfers between devices  102 us (12%)
  local copies, waits for them, and re-layouts  10.3 us (1%)
    dot_general x152, matrix products, transform(): lax.dot_general(vectors_in, matrix, (((1,), (1,)), ((), ())), precision=l...  175 us
    ppermute x38, waiting for transfers between devices, from_behind(): return lax.ppermute(block, axis, route)  148 us
    psum x1, blocking collectives, shards(): lax.psum(jnp.sum(first_solve * first_solve, axis=(0, 2)), 'chain')  129 us
    psum x1, blocking collectives, shards(): lax.psum(jnp.sum(second_solve * second_solve, axis=(0, 2)), 'chain')  129 us
    all_to_all x1, waiting for transfers between devices, shards(): lax.all_to_all(jnp.stack([factors] * lax.axis_size('cols')), 'cols', 0, 0)  96.2 us
    ppermute x38, starting transfers between devices, from_behind(): return lax.ppermute(block, axis, route)  91.9 us
    dot_general x42, matrix products, compose(): jnp.dot(later, earlier, precision=lax.Precision.HIGHEST, preferred_elemen...  46.4 us
  transfers between devices with their start and end apart: 39, of which 29 were waited for; matrix products, arithmetic and copies ran while one was open for 6% of the time, Pallas kernels for 0%

profile of v1, /device:TPU:32, one launch (start us, length us, event | category | flops | bytes accessed | tf_op | source)
XLA Modules:
  0.0 845.5 jit_solution(10647235117614062608)
XLA Ops:
  4.2 10.3 %all-to-all-start = ((f32[8,16,32,256]{3,2,1,0:T(8,128)}), f32[8,16,32,256]{3,2,1,0:T(8,128)}, u32[]{:S(2)}, u32[]{:S(2)}) async-start(f32[8,16,32,256]{3,2,1,0:T(8,128)} %stack.2), calls=%async_computation | async-start | bytes 8388608 | tf_op jit(solution)/shard_map/all_to_all | solution.py:82
  14.5 96.2 %all-to-all-done = f32[8,16,32,256]{3,2,1,0:T(8,128)} async-done(((f32[8,16,32,256]{3,2,1,0:T(8,128)}), f32[8,16,32,256]{3,2,1,0:T(8,128)}, u32[]{:S(2)}, u32[]{:S(2)}) %all-to-all-start) | async-done | bytes 4194336 | tf_op jit(solution)/shard_map/all_to_all | solution.py:82
  115.5 21.4 %while.146 = (s32[]{:T(128)}, f32[32,256]{1,0:T(8,128)S(1)}, f32[16,256,256]{2,1,0:T(8,128)}, f32[16,32,256]{2,1,0:T(8,128)}, s32[]{:T(128)}, /*index=5*/s32[]{:T(128)}) while((s32[]{:T(128)}, f32[32,256]{1,0:T(8,128)S(1)}, f32[16,256,256]{2,1,0:T(8,128)}, f32[16,32,256]{2,1,0:T(8,128)}, s32[]{:T(128)}, /*index=5*/s32[]{:T(128)}) %tuple.271), condition=%wide.region_1.2_spmd.clone, body=%wide.region_0.1_spmd.clone.sunk | while | flops 25182212 | bytes 427087 | solution.py:38
  138.8 22.1 %while.138 = (s32[]{:T(128)}, f32[256,256]{1,0:T(8,128)S(1)}, f32[16,256,256]{2,1,0:T(8,128)}, s32[]{:T(128)}) while((s32[]{:T(128)}, f32[256,256]{1,0:T(8,128)S(1)}, f32[16,256,256]{2,1,0:T(8,128)}, s32[]{:T(128)}) %tuple.272), condition=%wide.region_3.4_spmd, body=%wide.region_2.3_spmd.sunk | while | flops 201326592 | bytes 1311285 | solution.py:57
  177.4 7.2 collective-permute-done.4
  189.2 10.8 %collective-permute-done.6 = f32[256,256]{1,0:T(8,128)S(1)} collective-permute-done((f32[256,256]{1,0:T(8,128)S(1)}, f32[256,256]{1,0:T(8,128)S(1)}, u32[]{:S(2)}, u32[]{:S(2)}) %collective-permute-start.6) | collective-permute-done | bytes 262176 | tf_op jit(solution)/shard_map/ppermute | solution.py:12
  204.6 7.4 collective-permute-done.8
  216.0 7.5 collective-permute-done.10
  233.4 21.4 %while.139 = (s32[]{:T(128)}, f32[32,256]{1,0:T(8,128)S(1)}, f32[16,32,256]{2,1,0:T(8,128)S(1)}, f32[16,256,256]{2,1,0:T(8,128)}, f32[16,32,256]{2,1,0:T(8,128)}, /*index=5*/s32[]{:T(128)}) while((s32[]{:T(128)}, f32[32,256]{1,0:T(8,128)S(1)}, f32[16,32,256]{2,1,0:T(8,128)S(1)}, f32[16,256,256]{2,1,0:T(8,128)}, f32[16,32,256]{2,1,0:T(8,128)}, ...), condition=%wide.region_5.6_spmd, body=%wide.region_4.5_spmd.sunk | while | flops 25174016 | bytes 459845 | solution.py:38
  254.9 21.3 %while.140 = (s32[]{:T(128)}, f32[32,256]{1,0:T(8,128)S(1)}, f32[16,32,256]{2,1,0:T(8,128)S(1)}, f32[16,256,256]{2,1,0:T(8,128)}, s32[]{:T(128)}, /*index=5*/s32[]{:T(128)}) while((s32[]{:T(128)}, f32[32,256]{1,0:T(8,128)S(1)}, f32[16,32,256]{2,1,0:T(8,128)S(1)}, f32[16,256,256]{2,1,0:T(8,128)}, s32[]{:T(128)}, /*index=5*/s32[]{:T(128)}) %tuple.274), condition=%wide.region_7.8_spmd, body=%wide.region_6.7_spmd.sunk | while | flops 25174020 | bytes 427089 | solution.py:48
  278.1 22.1 %while.141 = (s32[]{:T(128)}, f32[256,256]{1,0:T(8,128)S(1)}, f32[16,256,256]{2,1,0:T(8,128)}, s32[]{:T(128)}, s32[]{:T(128)}) while((s32[]{:T(128)}, f32[256,256]{1,0:T(8,128)S(1)}, f32[16,256,256]{2,1,0:T(8,128)}, s32[]{:T(128)}, s32[]{:T(128)}) %tuple.275), condition=%wide.region_9.10_spmd, body=%wide.region_8.9_spmd.sunk | while | flops 201326592 | bytes 1310797 | solution.py:57
  321.2 7.5 collective-permute-done.18
  344.2 13.5 %collective-permute-done.22 = f32[256,256]{1,0:T(8,128)S(1)} collective-permute-done((f32[256,256]{1,0:T(8,128)S(1)}, f32[256,256]{1,0:T(8,128)S(1)}, u32[]{:S(2)}, u32[]{:S(2)}) %collective-permute-start.22) | collective-permute-done | bytes 262176 | tf_op jit(solution)/shard_map/ppermute | solution.py:12
  362.7 21.6 %while.142 = (s32[]{:T(128)}, f32[32,256]{1,0:T(8,128)S(1)}, f32[16,32,256]{2,1,0:T(8,128)S(1)}, f32[16,32,256]{2,1,0:T(8,128)}, f32[16,256,256]{2,1,0:T(8,128)}, /*index=5*/s32[]{:T(128)}, s32[]{:T(128)}) while((s32[]{:T(128)}, f32[32,256]{1,0:T(8,128)S(1)}, f32[16,32,256]{2,1,0:T(8,128)S(1)}, f32[16,32,256]{2,1,0:T(8,128)}, ...), condition=%wide.region_11.12_spmd, body=%wide.region_10.11_spmd.sunk | while | flops 25174020 | bytes 460377 | solution.py:48
  384.5 129.1 %psum.14 = f32[32]{0:T(128)S(1)} all-reduce(f32[32]{0:T(128)S(1)} %multiply_reduce_fusion.1), channel_id=1, replica_groups=mesh['chain'=64,'cols'=8] {'chain'}, use_global_device_ids=true, to_apply=%region_13.14 | all-reduce | flops 32 | bytes 256 | tf_op jit(solution)/shard_map/psum | solution.py:106
  514.6 21.5 %while.147 = (s32[]{:T(128)}, f32[32,256]{1,0:T(8,128)S(1)}, f32[16,256,256]{2,1,0:T(8,128)}, f32[16,32,256]{2,1,0:T(8,128)}, s32[]{:T(128)}, /*index=5*/s32[]{:T(128)}) while((s32[]{:T(128)}, f32[32,256]{1,0:T(8,128)S(1)}, f32[16,256,256]{2,1,0:T(8,128)}, f32[16,32,256]{2,1,0:T(8,128)}, s32[]{:T(128)}, ...), condition=%wide.region_15.16_spmd.clone, body=%wide.region_14.15_spmd.clone.sunk | while | flops 25182212 | bytes 427087 | solution.py:38
  546.8 7.2 collective-permute-done.25
  556.5 7.5 collective-permute-done.26
  581.2 8.4 collective-permute-done.29
  598.6 21.4 %while.143 = (s32[]{:T(128)}, f32[32,256]{1,0:T(8,128)S(1)}, f32[16,32,256]{2,1,0:T(8,128)S(1)}, f32[16,256,256]{2,1,0:T(8,128)}, f32[16,32,256]{2,1,0:T(8,128)}, /*index=5*/s32[]{:T(128)}) while((s32[]{:T(128)}, f32[32,256]{1,0:T(8,128)S(1)}, f32[16,32,256]{2,1,0:T(8,128)S(1)}, f32[16,256,256]{2,1,0:T(8,128)}, f32[16,32,256]{2,1,0:T(8,128)}, ...), condition=%wide.region_17.18_spmd, body=%wide.region_16.17_spmd.sunk | while | flops 25174016 | bytes 459845 | solution.py:38
  620.0 21.3 %while.144 = (s32[]{:T(128)}, f32[32,256]{1,0:T(8,128)S(1)}, f32[16,32,256]{2,1,0:T(8,128)S(1)}, f32[16,256,256]{2,1,0:T(8,128)}, s32[]{:T(128)}, /*index=5*/s32[]{:T(128)}) while((s32[]{:T(128)}, f32[32,256]{1,0:T(8,128)S(1)}, f32[16,32,256]{2,1,0:T(8,128)S(1)}, f32[16,256,256]{2,1,0:T(8,128)}, s32[]{:T(128)}, /*index=5*/s32[]{:T(128)}) %tuple.279), condition=%wide.region_19.20_spmd, body=%wide.region_18.19_spmd.sunk | while | flops 25174020 | bytes 427089 | solution.py:48
  675.6 16.3 %collective-permute-start.37 = (f32[32,256]{1,0:T(8,128)S(1)}, f32[32,256]{1,0:T(8,128)S(1)}, u32[]{:S(2)}, u32[]{:S(2)}) collective-permute-start(f32[32,256]{1,0:T(8,128)S(1)} %convolution_add_fusion), channel_id=1, source_target_pairs={{8,0},{16,8},{24,16},{32,24},{40,32},{48,40},{56,48},{64,56},{72,6... | collective-permute-start | bytes 98312 | tf_op jit(solution)/shard_map/ppermute | solution.py:12
  693.5 21.3 %while.145 = (s32[]{:T(128)}, f32[32,256]{1,0:T(8,128)S(1)}, f32[16,32,256]{2,1,0:T(8,128)S(1)}, f32[16,32,256]{2,1,0:T(8,128)S(1)}, f32[16,256,256]{2,1,0:T(8,128)}, /*index=5*/s32[]{:T(128)}, s32[]{:T(128)}) while((s32[]{:T(128)}, f32[32,256]{1,0:T(8,128)S(1)}, f32[16,32,256]{2,1,0:T(8,128)S(1)}, f32[16,32,256]{2,1,0:T(8,128)S(1)}, ...), condition=%wide.region_21.22_spmd, body=%wide.region_20.21_spmd.sunk | while | flops 25174020 | bytes 460377 | solution.py:48
  715.0 129.1 %psum.15 = f32[32]{0:T(128)S(1)} all-reduce(f32[32]{0:T(128)S(1)} %multiply_reduce_fusion), channel_id=1, replica_groups=mesh['chain'=64,'cols'=8] {'chain'}, use_global_device_ids=true, to_apply=%region_23.24 | all-reduce | flops 32 | bytes 256 | tf_op jit(solution)/shard_map/psum | solution.py:111
  (444 shorter events, 381.3 us)
Async XLA Ops:
  4.2 106.6 %all-to-all-start = ((f32[8,16,32,256]{3,2,1,0:T(8,128)}), f32[8,16,32,256]{3,2,1,0:T(8,128)}, u32[]{:S(2)}, u32[]{:S(2)}) async-start(f32[8,16,32,256]{3,2,1,0:T(8,128)} %stack.2), calls=%async_computation | async-start | bytes 8388608 | tf_op jit(solution)/shard_map/all_to_all | solution.py:82
  136.9 27.5 %collective-permute-start = (f32[32,256]{1,0:T(8,128)S(1)}, f32[32,256]{1,0:T(8,128)S(1)}, u32[]{:S(2)}, u32[]{:S(2)}) collective-permute-start(f32[32,256]{1,0:T(8,128)S(1)} %get-tuple-element.568), channel_id=1, source_target_pairs={{0,8},{8,16},{16,24},{24,32},{32,40},{40,48},{48,56},{56,64},{64,7... | collective-permute-start | bytes 98312 | tf_op jit(solution)/shard_map/ppermute | solution.py:12
  160.9 11.0 %collective-permute-start.2 = (f32[256,256]{1,0:T(8,128)S(1)}, f32[256,256]{1,0:T(8,128)S(1)}, u32[]{:S(2)}, u32[]{:S(2)}) collective-permute-start(f32[256,256]{1,0:T(8,128)S(1)} %get-tuple-element.569), channel_id=1, source_target_pairs={{0,8},{8,16},{16,24},{24,32},{32,40},{40,48},{48,56},{56,64},{64,7... | collective-permute-start | bytes 786440 | tf_op jit(solution)/shard_map/ppermute | solution.py:12
  164.8 9.5 %collective-permute-start.1 = (f32[32,256]{1,0:T(8,128)S(1)}, f32[32,256]{1,0:T(8,128)S(1)}, u32[]{:S(2)}, u32[]{:S(2)}) collective-permute-start(f32[32,256]{1,0:T(8,128)S(1)} %convolution_add_fusion.23), channel_id=1, source_target_pairs={{0,16},{8,24},{16,32},{24,40},{32,48},{40,56},{48,64},{56,72},{64,... | collective-permute-start | bytes 98312 | tf_op jit(solution)/shard_map/ppermute | solution.py:12
  172.3 12.3 %collective-permute-start.4 = (f32[256,256]{1,0:T(8,128)S(1)}, f32[256,256]{1,0:T(8,128)S(1)}, u32[]{:S(2)}, u32[]{:S(2)}) collective-permute-start(f32[256,256]{1,0:T(8,128)S(1)} %fusion.54), channel_id=1, source_target_pairs={{0,16},{8,24},{16,32},{24,40},{32,48},{40,56},{48,64},{56,72},{64,... | collective-permute-start | bytes 786440 | tf_op jit(solution)/shard_map/ppermute | solution.py:12
  174.6 12.3 %collective-permute-start.3 = (f32[32,256]{1,0:T(8,128)S(1)}, f32[32,256]{1,0:T(8,128)S(1)}, u32[]{:S(2)}, u32[]{:S(2)}) collective-permute-start(f32[32,256]{1,0:T(8,128)S(1)} %convolution_add_fusion.22), channel_id=1, source_target_pairs={{0,32},{8,40},{16,48},{24,56},{32,64},{40,72},{48,80},{56,88},{64,... | collective-permute-start | bytes 98312 | tf_op jit(solution)/shard_map/ppermute | solution.py:12
  185.0 15.0 %collective-permute-start.6 = (f32[256,256]{1,0:T(8,128)S(1)}, f32[256,256]{1,0:T(8,128)S(1)}, u32[]{:S(2)}, u32[]{:S(2)}) collective-permute-start(f32[256,256]{1,0:T(8,128)S(1)} %fusion.55), channel_id=1, source_target_pairs={{0,32},{8,40},{16,48},{24,56},{32,64},{40,72},{48,80},{56,88},{64,... | collective-permute-start | bytes 786440 | tf_op jit(solution)/shard_map/ppermute | solution.py:12
  187.3 15.1 %collective-permute-start.5 = (f32[32,256]{1,0:T(8,128)S(1)}, f32[32,256]{1,0:T(8,128)S(1)}, u32[]{:S(2)}, u32[]{:S(2)}) collective-permute-start(f32[32,256]{1,0:T(8,128)S(1)} %convolution_add_fusion.21), channel_id=1, source_target_pairs={{0,64},{8,72},{16,80},{24,88},{32,96},{40,104},{48,112},{56,120},{... | collective-permute-start | bytes 98312 | tf_op jit(solution)/shard_map/ppermute | solution.py:12
  200.4 11.6 %collective-permute-start.8 = (f32[256,256]{1,0:T(8,128)S(1)}, f32[256,256]{1,0:T(8,128)S(1)}, u32[]{:S(2)}, u32[]{:S(2)}) collective-permute-start(f32[256,256]{1,0:T(8,128)S(1)} %fusion.56), channel_id=1, source_target_pairs={{0,64},{8,72},{16,80},{24,88},{32,96},{40,104},{48,112},{56,120},{... | collective-permute-start | bytes 786440 | tf_op jit(solution)/shard_map/ppermute | solution.py:12
  202.7 11.7 %collective-permute-start.7 = (f32[32,256]{1,0:T(8,128)S(1)}, f32[32,256]{1,0:T(8,128)S(1)}, u32[]{:S(2)}, u32[]{:S(2)}) collective-permute-start(f32[32,256]{1,0:T(8,128)S(1)} %convolution_add_fusion.20), channel_id=1, source_target_pairs={{0,128},{8,136},{16,144},{24,152},{32,160},{40,168},{48,176},{56,1... | collective-permute-start | bytes 98312 | tf_op jit(solution)/shard_map/ppermute | solution.py:12
  212.4 11.0 %collective-permute-start.10 = (f32[256,256]{1,0:T(8,128)S(1)}, f32[256,256]{1,0:T(8,128)S(1)}, u32[]{:S(2)}, u32[]{:S(2)}) collective-permute-start(f32[256,256]{1,0:T(8,128)S(1)} %fusion.57), channel_id=1, source_target_pairs={{0,128},{8,136},{16,144},{24,152},{32,160},{40,168},{48,176},{56,1... | collective-permute-start | bytes 786440 | tf_op jit(solution)/shard_map/ppermute | solution.py:12
  214.7 9.7 %collective-permute-start.9 = (f32[32,256]{1,0:T(8,128)S(1)}, f32[32,256]{1,0:T(8,128)S(1)}, u32[]{:S(2)}, u32[]{:S(2)}) collective-permute-start(f32[32,256]{1,0:T(8,128)S(1)} %convolution_add_fusion.19), channel_id=1, source_target_pairs={{0,256},{8,264},{16,272},{24,280},{32,288},{40,296},{48,304},{56,3... | collective-permute-start | bytes 98312 | tf_op jit(solution)/shard_map/ppermute | solution.py:12
  276.2 26.0 %collective-permute-start.12 = (f32[32,256]{1,0:T(8,128)S(1)}, f32[32,256]{1,0:T(8,128)S(1)}, u32[]{:S(2)}, u32[]{:S(2)}) collective-permute-start(f32[32,256]{1,0:T(8,128)S(1)} %get-tuple-element.571), channel_id=1, source_target_pairs={{8,0},{16,8},{24,16},{32,24},{40,32},{48,40},{56,48},{64,56},{72,6... | collective-permute-start | bytes 98312 | tf_op jit(solution)/shard_map/ppermute | solution.py:12
  306.8 9.8 %collective-permute-start.16 = (f32[256,256]{1,0:T(8,128)S(1)}, f32[256,256]{1,0:T(8,128)S(1)}, u32[]{:S(2)}, u32[]{:S(2)}) collective-permute-start(f32[256,256]{1,0:T(8,128)S(1)} %fusion.59), channel_id=1, source_target_pairs={{16,0},{24,8},{32,16},{40,24},{48,32},{56,40},{64,48},{72,56},{80,... | collective-permute-start | bytes 786440 | tf_op jit(solution)/shard_map/ppermute | solution.py:12
  309.7 9.2 %collective-permute-start.15 = (f32[32,256]{1,0:T(8,128)S(1)}, f32[32,256]{1,0:T(8,128)S(1)}, u32[]{:S(2)}, u32[]{:S(2)}) collective-permute-start(f32[32,256]{1,0:T(8,128)S(1)} %convolution_add_fusion.16), channel_id=1, source_target_pairs={{32,0},{40,8},{48,16},{56,24},{64,32},{72,40},{80,48},{88,56},{96,... | collective-permute-start | bytes 98312 | tf_op jit(solution)/shard_map/ppermute | solution.py:12
  317.0 11.7 %collective-permute-start.18 = (f32[256,256]{1,0:T(8,128)S(1)}, f32[256,256]{1,0:T(8,128)S(1)}, u32[]{:S(2)}, u32[]{:S(2)}) collective-permute-start(f32[256,256]{1,0:T(8,128)S(1)} %fusion.60), channel_id=1, source_target_pairs={{32,0},{40,8},{48,16},{56,24},{64,32},{72,40},{80,48},{88,56},{96,... | collective-permute-start | bytes 786440 | tf_op jit(solution)/shard_map/ppermute | solution.py:12
  319.3 12.0 %collective-permute-start.17 = (f32[32,256]{1,0:T(8,128)S(1)}, f32[32,256]{1,0:T(8,128)S(1)}, u32[]{:S(2)}, u32[]{:S(2)}) collective-permute-start(f32[32,256]{1,0:T(8,128)S(1)} %convolution_add_fusion.15), channel_id=1, source_target_pairs={{64,0},{72,8},{80,16},{88,24},{96,32},{104,40},{112,48},{120,56},{... | collective-permute-start | bytes 98312 | tf_op jit(solution)/shard_map/ppermute | solution.py:12
  329.0 11.2 %collective-permute-start.20 = (f32[256,256]{1,0:T(8,128)S(1)}, f32[256,256]{1,0:T(8,128)S(1)}, u32[]{:S(2)}, u32[]{:S(2)}) collective-permute-start(f32[256,256]{1,0:T(8,128)S(1)} %fusion.61), channel_id=1, source_target_pairs={{64,0},{72,8},{80,16},{88,24},{96,32},{104,40},{112,48},{120,56},{... | collective-permute-start | bytes 786440 | tf_op jit(solution)/shard_map/ppermute | solution.py:12
  331.6 11.0 %collective-permute-start.19 = (f32[32,256]{1,0:T(8,128)S(1)}, f32[32,256]{1,0:T(8,128)S(1)}, u32[]{:S(2)}, u32[]{:S(2)}) collective-permute-start(f32[32,256]{1,0:T(8,128)S(1)} %convolution_add_fusion.14), channel_id=1, source_target_pairs={{128,0},{136,8},{144,16},{152,24},{160,32},{168,40},{176,48},{184,... | collective-permute-start | bytes 98312 | tf_op jit(solution)/shard_map/ppermute | solution.py:12
  340.6 17.1 %collective-permute-start.22 = (f32[256,256]{1,0:T(8,128)S(1)}, f32[256,256]{1,0:T(8,128)S(1)}, u32[]{:S(2)}, u32[]{:S(2)}) collective-permute-start(f32[256,256]{1,0:T(8,128)S(1)} %fusion.62), channel_id=1, source_target_pairs={{128,0},{136,8},{144,16},{152,24},{160,32},{168,40},{176,48},{184,... | collective-permute-start | bytes 786440 | tf_op jit(solution)/shard_map/ppermute | solution.py:12
  342.9 15.2 %collective-permute-start.21 = (f32[32,256]{1,0:T(8,128)S(1)}, f32[32,256]{1,0:T(8,128)S(1)}, u32[]{:S(2)}, u32[]{:S(2)}) collective-permute-start(f32[32,256]{1,0:T(8,128)S(1)} %convolution_add_fusion.13), channel_id=1, source_target_pairs={{256,0},{264,8},{272,16},{280,24},{288,32},{296,40},{304,48},{312,... | collective-permute-start | bytes 98312 | tf_op jit(solution)/shard_map/ppermute | solution.py:12
  554.4 9.6 %collective-permute-start.26 = (f32[32,256]{1,0:T(8,128)S(1)}, f32[32,256]{1,0:T(8,128)S(1)}, u32[]{:S(2)}, u32[]{:S(2)}) collective-permute-start(f32[32,256]{1,0:T(8,128)S(1)} %convolution_add_fusion.10), channel_id=1, source_target_pairs={{0,32},{8,40},{16,48},{24,56},{32,64},{40,72},{48,80},{56,88},{64,... | collective-permute-start | bytes 98312 | tf_op jit(solution)/shard_map/ppermute | solution.py:12
  579.9 9.7 %collective-permute-start.29 = (f32[32,256]{1,0:T(8,128)S(1)}, f32[32,256]{1,0:T(8,128)S(1)}, u32[]{:S(2)}, u32[]{:S(2)}) collective-permute-start(f32[32,256]{1,0:T(8,128)S(1)} %convolution_add_fusion.7), channel_id=1, source_target_pairs={{0,256},{8,264},{16,272},{24,280},{32,288},{40,296},{48,304},{56,3... | collective-permute-start | bytes 98312 | tf_op jit(solution)/shard_map/ppermute | solution.py:12
  675.6 17.8 %collective-permute-start.37 = (f32[32,256]{1,0:T(8,128)S(1)}, f32[32,256]{1,0:T(8,128)S(1)}, u32[]{:S(2)}, u32[]{:S(2)}) collective-permute-start(f32[32,256]{1,0:T(8,128)S(1)} %convolution_add_fusion), channel_id=1, source_target_pairs={{8,0},{16,8},{24,16},{32,24},{40,32},{48,40},{56,48},{64,56},{72,6... | collective-permute-start | bytes 98312 | tf_op jit(solution)/shard_map/ppermute | solution.py:12
  (18 other events, 248.3 us)
